TPU v7x, 128 devices: a whole 4x4x4 slice. The times are simulated.
128 devices in a mesh: req: 8 (over y, core), tok: 16 (over x, z).
Axes of the slice: x: 4, y: 4, z: 4, core: 2. Of those that a mesh axis runs over, the one named last changes fastest.
Arguments:
- layer_input: bfloat16 [16384, 2048], P(('req', 'tok')), may hold values from -12 to 12
- q_in: bfloat16 [16384, 2048], P(('req', 'tok')), may hold values from -10 to 10
- k_in: bfloat16 [16384, 2048], P(('req', 'tok')), may hold values from -10 to 10
- v_in: bfloat16 [16384, 2048], P(('req', 'tok')), may hold values from -6 to 6
- segment_ids: int32 [8, 2048], P('req'), may hold values from 0 to 3, never falling along the last dimension, each value on 1 to 1024 neighbouring positions
- lambda_parts: float32 [4, 128], replicated, may hold values from -0.8 to 0.8
- out_weight: bfloat16 [2048, 2048], replicated, may hold values from -0.125 to 0.125
- ffn_gain: float32 [2048], replicated, may hold values from 0.1 to 1.9
- gate_weight: bfloat16 [2048, 5632], P(None, 'req'), may hold values from -0.125 to 0.125
- up_weight: bfloat16 [2048, 5632], P(None, 'req'), may hold values from -0.125 to 0.125
- down_weight: bfloat16 [5632, 2048], P('req'), may hold values from -0.078125 to 0.078125
- next_gain: float32 [2048], replicated, may hold values from 0.1 to 1.9
- qkv_weight: bfloat16 [2048, 6144], P(None, 'req'), may hold values from -0.125 to 0.125
- page_owner: int32 [8, 256], P('req'), may hold values from 0 to 15, as said below
- page_slot: int32 [8, 256], P('req'), may hold values from 0 to 15, as said below
Outputs:
- layer_output: bfloat16 [16384, 2048], P(('req', 'tok'))
- q_next: bfloat16 [16384, 2048], P(('req', 'tok'))
- page_cache: bfloat16 [2048, 8, 4096], P(('req', 'tok'))
Inputs may be any that keep to these rules, and one draw needn't show every extreme that they name: `segment_ids`: segment numbers never fall along a group; each of the 4 prompts of a group has 1 to 1024 tokens, one exactly 1024. `page_owner`: the 16 pages of each device name every device of its request group as owner exactly once. `page_slot`: within a request group every pair of owner and slot is named by exactly one page.
All inputs are finite; a program needn't handle non-finite values.
Results may differ from a plain program's by a relative error of at most 0.017.
Values may be sent and summed in bfloat16 or wider, within the bound.
A program may use at most 192 MiB of HBM per device.

v0:
```python
import math
import jax
import jax.numpy as jnp
from jax import lax
from jax.sharding import PartitionSpec as P

HEADS = 8
PAGE = 8
NEG_FILL = -1e30
LAMBDA_INIT = 0.2
EPSILON = 1e-05


def rms_rows(values):
    return values * lax.rsqrt(jnp.mean(values * values, axis=-1, keepdims=True) + EPSILON)


def lambda_value(lambda_parts):
    first_term = jnp.exp(jnp.sum(lambda_parts[0] * lambda_parts[1]))
    second_term = jnp.exp(jnp.sum(lambda_parts[2] * lambda_parts[3]))
    return first_term - second_term + LAMBDA_INIT


def body(
    layer_input,
    q_in,
    k_in,
    v_in,
    segment_ids,
    lambda_parts,
    out_weight,
    ffn_gain,
    gate_weight,
    up_weight,
    down_weight,
    next_gain,
    qkv_weight,
    page_owner,
    page_slot,
):
    row_count = q_in.shape[0]
    feat_width = q_in.shape[1]
    head_dim = feat_width // (2 * HEADS)
    peer_count = lax.axis_size("tok")
    tok_place = lax.axis_index("tok")
    seg_row = segment_ids[0]
    first_row = tok_place * row_count
    query_places = first_row + jnp.arange(row_count)
    query_segs = lax.dynamic_slice_in_dim(seg_row, first_row, row_count)
    lambda_mix = lambda_value(lambda_parts)
    score_scale = 1.0 / math.sqrt(head_dim)
    query_split = q_in.reshape(row_count, HEADS, 2, head_dim)
    run_max = jnp.full((HEADS, 2, row_count), NEG_FILL, jnp.float32)
    key_rows = lax.all_gather(k_in, "tok", axis=0, tiled=True)
    value_rows = lax.all_gather(v_in, "tok", axis=0, tiled=True)
    piece_len = key_rows.shape[0]
    key_split = key_rows.reshape(piece_len, HEADS, 2, head_dim)
    value_split = value_rows.reshape(piece_len, HEADS, 2 * head_dim)
    key_places = jnp.arange(piece_len)
    visible = (seg_row[None, :] == query_segs[:, None]) & (
        key_places[None, :] <= query_places[:, None]
    )
    scores = (
        jnp.einsum("qhmd,khmd->hmqk", query_split, key_split, preferred_element_type=jnp.float32)
        * score_scale
    )
    scores = jnp.where(visible, scores, NEG_FILL)
    new_max = jnp.maximum(run_max, jnp.max(scores, axis=-1))
    weights = jnp.where(visible, jnp.exp(scores - new_max[..., None]), 0.0)
    totals = jnp.sum(weights, axis=-1)
    weighted = jnp.einsum(
        "hmqk,khe->hmqe",
        weights.astype(jnp.bfloat16),
        value_split,
        preferred_element_type=jnp.float32,
    )
    run_max, totals, weighted = (new_max, totals, weighted)
    map_outputs = weighted / totals[..., None]
    difference = map_outputs[:, 0] - lambda_mix * map_outputs[:, 1]
    head_outputs = rms_rows(difference) * (1.0 - LAMBDA_INIT)
    attention = (
        jnp.transpose(head_outputs, (1, 0, 2)).reshape(row_count, feat_width).astype(jnp.bfloat16)
    )
    residual_mid = (
        layer_input.astype(jnp.float32)
        + jnp.dot(attention, out_weight, preferred_element_type=jnp.float32)
    ).astype(jnp.bfloat16)
    gathered = lax.all_gather(residual_mid, "req", axis=0, tiled=True)
    normed = (rms_rows(gathered.astype(jnp.float32)) * ffn_gain).astype(jnp.bfloat16)
    gate_proj = jnp.dot(normed, gate_weight, preferred_element_type=jnp.float32)
    up_proj = jnp.dot(normed, up_weight, preferred_element_type=jnp.float32)
    hidden = (jax.nn.silu(gate_proj) * up_proj).astype(jnp.bfloat16)
    ffn_own = lax.psum_scatter(
        jnp.dot(hidden, down_weight, preferred_element_type=jnp.float32).astype(jnp.bfloat16),
        "req",
        scatter_dimension=0,
        tiled=True,
    ).astype(jnp.float32)
    layer_output = (residual_mid.astype(jnp.float32) + ffn_own).astype(jnp.bfloat16)
    next_normed = (rms_rows(layer_output.astype(jnp.float32)) * next_gain).astype(jnp.bfloat16)
    projected_cols = jnp.dot(
        lax.all_gather(next_normed, "req", axis=0, tiled=True),
        qkv_weight,
        preferred_element_type=jnp.float32,
    ).astype(jnp.bfloat16)
    projected = lax.all_to_all(projected_cols, "req", split_axis=0, concat_axis=1, tiled=True)
    q_next = projected[:, :feat_width]
    pages_dev = row_count // PAGE
    per_owner = pages_dev // peer_count
    key_values = projected[:, feat_width:].reshape(pages_dev, PAGE, 2 * feat_width)
    owner_all = page_owner[0].reshape(peer_count, pages_dev)
    slot_all = page_slot[0].reshape(peer_count, pages_dev)
    page_numbers = jnp.arange(pages_dev, dtype=jnp.int32)
    my_owners = lax.dynamic_index_in_dim(owner_all, tok_place, 0, keepdims=False)
    send_order = jnp.argsort(my_owners * pages_dev + page_numbers)
    outgoing = key_values[send_order].reshape(peer_count, per_owner, PAGE, 2 * feat_width)
    incoming = lax.all_to_all(outgoing, "tok", split_axis=0, concat_axis=0, tiled=True)
    rank_keys = jnp.where(
        owner_all == tok_place, page_numbers[None, :], pages_dev + page_numbers[None, :]
    )
    chosen_pages = jnp.argsort(rank_keys, axis=1)[:, :per_owner]
    slot_list = jnp.take_along_axis(slot_all, chosen_pages, axis=1).reshape(pages_dev)
    page_cache = (
        jnp.zeros((pages_dev, PAGE, 2 * feat_width), jnp.bfloat16)
        .at[slot_list]
        .set(incoming.reshape(pages_dev, PAGE, 2 * feat_width))
    )
    return (layer_output, q_next, page_cache)


def solution(mesh):
    in_specs = (
        P(("req", "tok"), None),
        P(("req", "tok"), None),
        P(("req", "tok"), None),
        P(("req", "tok"), None),
        P("req", None),
        P(),
        P(),
        P(),
        P(None, "req"),
        P(None, "req"),
        P("req", None),
        P(),
        P(None, "req"),
        P("req", None),
        P("req", None),
    )
    out_specs = (P(("req", "tok"), None), P(("req", "tok"), None), P(("req", "tok"), None, None))
    return jax.shard_map(body, mesh=mesh, in_specs=in_specs, out_specs=out_specs, check_vma=False)
```

profile of v0, /device:TPU:0, one launch (start us, length us, event | category | flops | bytes accessed | tf_op | source)
XLA Modules:
  0.0 395.1 jit_solution(589856986905657744)
XLA Ops:
  7.2 0.0 copy-start
  7.2 0.0 copy-start.7
  7.2 0.0 all-gather.5.cloned.1.call-start
  7.2 2.2 copy.35
  9.4 0.0 all-gather.5.cloned.1.call-update
  9.5 0.0 all-gather.7.cloned.1.call-start
  9.5 2.0 copy.38
  11.6 0.0 all-gather.7.cloned.1.call-update
  11.6 0.0 all-gather.9.cloned.1.call-start
  11.6 2.2 reshape.96
  13.8 0.0 copy-done.7
  13.8 0.6 multiply_reduce_fusion.1
  15.8 0.4 fusion.24
  16.2 75.5 %all-gather.5.cloned.1.call-done = bf16[2048,2048]{0,1:T(8,128)(2,1)} async-done(((bf16[128,2048]{0,1:T(8,128)(2,1)}), bf16[2048,2048]{0,1:T(8,128)(2,1)}) %all-gather.5.cloned.1.call-update) | async-done | bytes 8388624 | tf_op jit(solution)/shard_map/all_gather | solution.py:54
  91.7 6.6 %fusion = (f32[8,2,128]{2,1,0:T(2,128)S(1)}, f32[8,2,128,2048]{3,2,1,0:T(8,128)S(1)}) fusion(pred[128,2048]{1,0:T(8,128)(4,1)S(1)} %fusion.24, bf16[2048,8,2,128]{0,3,2,1:T(8,128)(2,1)} %bitcast.49, bf16[128,8,2,128]{3,2,1,0:T(2,128)(2,1)} %reshape.96), kind=kOutput, calls=%fused_computation.5 | convolution fusion | flops 1086322688 | bytes 25960448 | tf_op jit(solution)/shard_map/qhmd,khmd->hmqk/dot_general | solution.py:64
  98.4 0.0 copy-start.1
  98.4 5.9 %copy-done.1 = f32[8,2,128,2048]{3,2,1,0:T(8,128)} copy-done((f32[8,2,128,2048]{3,2,1,0:T(8,128)}, f32[8,2,128,2048]{3,2,1,0:T(8,128)S(1)}, u32[]{:S(2)}) %copy-start.1) | copy-done | bytes 16777240
  104.3 5.0 %fusion.1 = f32[8,2,128]{2,1,0:T(2,128)S(1)} fusion(f32[8,2,128,2048]{3,2,1,0:T(8,128)S(1)} %get-tuple-element.12, f32[8,2,128]{2,1,0:T(2,128)S(1)} %broadcast_maximum_fusion, pred[128,2048]{1,0:T(8,128)(4,1)S(1)} %fusion.24), kind=kLoop, calls=%fused_computation.6 | loop fusion | flops 20969472 | bytes 17055744 | tf_op jit(solution)/shard_map/reduce_sum | solution.py:70
  109.3 63.0 %all-gather.7.cloned.1.call-done = bf16[2048,2048]{0,1:T(8,128)(2,1)} async-done(((bf16[128,2048]{0,1:T(8,128)(2,1)}), bf16[2048,2048]{0,1:T(8,128)(2,1)}) %all-gather.7.cloned.1.call-update) | async-done | bytes 8388624 | tf_op jit(solution)/shard_map/all_gather | solution.py:55
  172.3 12.6 %broadcast_divide_fusion = f32[8,2,128,256]{3,2,1,0:T(8,128)S(1)} fusion(f32[8,2,128]{2,1,0:T(2,128)S(1)} %fusion.1, bf16[2048,8,256,1]{0,2,3,1:T(8,128)(2,1)} %bitcast.56, f32[8,2,128,2048]{3,2,1,0:T(8,128)} %copy-done.1, f32[8,2,128]{2,1,0:T(2,128)S(1)} %broadcast_maximum_fusion, pred[128,2048]{1,0:T(8,128)(4,1)S(1)} %fusion.24), kind=kOutput, calls=%fused_computation.37 | convolution fusion | flops 2168979456 | bytes 27541504 | tf_op jit(solution)/shard_map/hmqk,khe->hmqe/dot_general | solution.py:71
  184.9 0.2 multiply_reduce_fusion
  185.1 1.1 fusion.25
  186.2 2.0 copy.40
  188.3 5.7 %fusion.13 = bf16[128,2048]{1,0:T(8,128)(2,1)} fusion(bf16[128,2048]{0,1:T(8,128)(2,1)} %bitcast.53, bf16[2048,2048]{1,0:T(8,128)(2,1)} %param.21, bf16[128,2048]{1,0:T(8,128)(2,1)} %param.15), kind=kOutput, calls=%fused_computation.22 | convolution fusion | flops 1074528256 | bytes 9961472 | tf_op jit(solution)/shard_map/dot_general | solution.py:86
  193.9 0.0 all-gather.9.cloned.1.call-update
  193.9 0.2 reduce-scatter.2.cloned.1.call-start
  194.2 31.3 %all-gather.9.cloned.1.call-done = bf16[1024,2048]{1,0:T(8,128)(2,1)} async-done(((bf16[128,2048]{1,0:T(8,128)(2,1)}), bf16[1024,2048]{1,0:T(8,128)(2,1)}) %all-gather.9.cloned.1.call-update) | async-done | bytes 4194320 | tf_op jit(solution)/shard_map/all_gather | solution.py:88
  225.5 3.2 fusion.3
  228.7 0.0 copy-done.10
  228.7 0.2 copy-done.3
  228.9 6.7 %fusion.15 = f32[1024,704]{0,1:T(8,128)} fusion(bf16[2048,704]{0,1:T(8,128)(2,1)} %param.23, bf16[1024,2048]{1,0:T(8,128)(2,1)S(1)} %copy-done.3, f32[2048]{0:T(1024)S(1)} %copy-done.10, f32[1024]{0:T(1024)S(1)} %add_rsqrt_fusion), kind=kOutput, calls=%fused_computation.26 | convolution fusion | flops 2961178624 | bytes 9973760 | tf_op jit(solution)/shard_map/dot_general | solution.py:90
  235.7 12.4 %convolution_convert_fusion = bf16[1024,2048]{1,0:T(8,128)(2,1)} fusion(bf16[704,2048]{1,0:T(8,128)(2,1)} %param.25, f32[1024,704]{0,1:T(8,128)} %fusion.15, bf16[2048,704]{0,1:T(8,128)(2,1)} %param.24, bf16[1024,2048]{1,0:T(8,128)(2,1)} %all-gather.9.cloned.1.call-done, f32[2048]{0:T(1024)S(1)} %copy-done.10, f32[1024]{0:T(1024)S(1)} %add_rsqrt_fusion), kind=kOutput, calls=%fused_computation.19 | convolution fusion | flops 5920391168 | bytes 17051648 | tf_op jit(solution)/shard_map/dot_general | solution.py:94
  248.1 0.0 reduce-scatter.2.cloned.1.call-update
  248.1 0.0 all-gather.11.cloned.1.call-start
  248.1 37.9 %reduce-scatter.2.cloned.1.call-done = bf16[128,2048]{1,0:T(8,128)(2,1)} async-done(((bf16[1024,2048]{1,0:T(8,128)(2,1)}), bf16[128,2048]{1,0:T(8,128)(2,1)}) %reduce-scatter.2.cloned.1.call-update) | async-done | bytes 524304 | tf_op jit(solution)/shard_map/reduce_scatter | solution.py:93
  286.0 1.5 fusion.19
  287.5 0.8 copy-done.4
  288.3 1.0 fusion.21
  289.2 0.0 all-gather.11.cloned.1.call-update
  289.3 0.0 copy-start.8
  289.3 0.0 copy-start.9
  289.3 31.2 %all-gather.11.cloned.1.call-done = bf16[1024,2048]{1,0:T(8,128)(2,1)} async-done(((bf16[128,2048]{1,0:T(8,128)(2,1)}), bf16[1024,2048]{1,0:T(8,128)(2,1)}) %all-gather.11.cloned.1.call-update) | async-done | bytes 4194320 | tf_op jit(solution)/shard_map/all_gather | solution.py:102
  320.4 6.8 %convolution_convert_fusion.1 = bf16[1024,768]{1,0:T(8,128)(2,1)} fusion(bf16[1024,2048]{1,0:T(8,128)(2,1)} %all-gather.11.cloned.1.call-done, bf16[2048,768]{1,0:T(8,128)(2,1)S(1)} %copy-done), kind=kOutput, calls=%fused_computation.23 | convolution fusion | flops 3222011904 | bytes 8912896 | tf_op jit(solution)/shard_map/dot_general | solution.py:101
  327.2 4.3 %all-to-all-start = ((bf16[8,128,768]{2,1,0:T(8,128)(2,1)}), bf16[8,128,768]{2,1,0:T(8,128)(2,1)}, u32[]{:S(2)}, u32[]{:S(2)}) async-start(bf16[8,128,768]{2,1,0:T(8,128)(2,1)} %bitcast.54), calls=%async_computation.1 | async-start | bytes 3145728 | tf_op jit(solution)/shard_map/all_to_all | solution.py:106
  331.5 0.5 broadcast.117
  332.0 0.7 reduce.9
  332.7 0.1 reshape_squeeze.6
  332.8 0.1 copy.42
  332.9 0.7 reduce.8
  333.5 0.1 reshape_squeeze.7
  333.6 1.2 sort.35
  334.9 18.2 %all-to-all-done = bf16[8,128,768]{2,1,0:T(8,128)(2,1)} async-done(((bf16[8,128,768]{2,1,0:T(8,128)(2,1)}), bf16[8,128,768]{2,1,0:T(8,128)(2,1)}, u32[]{:S(2)}, u32[]{:S(2)}) %all-to-all-start) | async-done | bytes 1572896 | tf_op jit(solution)/shard_map/all_to_all | solution.py:106
  353.1 1.6 copy.47
  354.7 1.1 copy-done.2
  355.8 1.0 slice_bitcast_fusion
  356.9 2.8 gather_fusion
  359.7 7.0 %all-to-all-start.1 = ((bf16[16,1,8,4096]{3,2,1,0:T(8,128)(2,1)}), bf16[16,1,8,4096]{3,2,1,0:T(8,128)(2,1)}, u32[]{:S(2)}, u32[]{:S(2)}) async-start(bf16[16,1,8,4096]{3,2,1,0:T(8,128)(2,1)} %bitcast.52), calls=%async_computation.2 | async-start | bytes 2097152 | tf_op jit(solution)/shard_map/all_to_all | solution.py:117
  366.7 0.1 iota_select_fusion
  366.8 0.7 sort.34
  367.5 0.7 gather_fusion.1
  368.2 1.9 slice.42
  370.1 14.1 %all-to-all-done.1 = bf16[16,1,8,4096]{3,2,1,0:T(8,128)(2,1)} async-done(((bf16[16,1,8,4096]{3,2,1,0:T(8,128)(2,1)}), bf16[16,1,8,4096]{3,2,1,0:T(8,128)(2,1)}, u32[]{:S(2)}, u32[]{:S(2)}) %all-to-all-start.1) | async-done | bytes 1048608 | tf_op jit(solution)/shard_map/all_to_all | solution.py:117
  384.1 1.1 broadcast_in_dim.54
  385.2 3.4 scatter_fusion
  (28 shorter events, 0.1 us)
Async XLA Ops:
  7.2 313.3 %copy-start = (bf16[2048,768]{1,0:T(8,128)(2,1)S(1)}, bf16[2048,768]{1,0:T(8,128)(2,1)}, u32[]{:S(2)}) copy-start(bf16[2048,768]{1,0:T(8,128)(2,1)} %param.27) | copy-start | bytes 9437188
  7.2 6.7 %copy-start.7 = (f32[4,128]{1,0:T(4,128)S(1)}, f32[4,128]{1,0:T(4,128)}, u32[]{:S(2)}) copy-start(f32[4,128]{1,0:T(4,128)} %param.20) | copy-start | bytes 6148
  7.2 8.6 %copy-start.6 = (s32[1,2048]{1,0:T(1,128)S(1)}, s32[1,2048]{1,0:T(1,128)}, u32[]{:S(2)}) copy-start(s32[1,2048]{1,0:T(1,128)} %param.19) | copy-start | bytes 24580
  7.2 84.5 %all-gather.5.cloned.1.call-start = ((), (), s32[]{:S(2)}) async-start(), calls=%async_computation.3 | async-start | bytes 8912896 | tf_op jit(solution)/shard_map/all_gather | solution.py:54
  9.5 162.8 %all-gather.7.cloned.1.call-start = ((), (), s32[]{:S(2)}) async-start(), calls=%async_computation.4 | async-start | bytes 8912896 | tf_op jit(solution)/shard_map/all_gather | solution.py:55
  11.6 213.9 %all-gather.9.cloned.1.call-start = ((), (), s32[]{:S(2)}) async-start(), calls=%async_computation.5 | async-start | bytes 4718592 | tf_op jit(solution)/shard_map/all_gather | solution.py:88
  98.4 5.9 %copy-start.1 = (f32[8,2,128,2048]{3,2,1,0:T(8,128)}, f32[8,2,128,2048]{3,2,1,0:T(8,128)S(1)}, u32[]{:S(2)}) copy-start(f32[8,2,128,2048]{3,2,1,0:T(8,128)S(1)} %get-tuple-element.12) | copy-start | bytes 50331652
  193.9 34.8 %copy-start.10 = (f32[2048]{0:T(1024)S(1)}, f32[2048]{0:T(1024)}, u32[]{:S(2)}) copy-start(f32[2048]{0:T(1024)} %param.22) | copy-start | bytes 24580
  193.9 92.0 %reduce-scatter.2.cloned.1.call-start = ((), (), s32[]{:S(2)}) async-start(), calls=%async_computation.6 | async-start | bytes 4718592 | tf_op jit(solution)/shard_map/reduce_scatter | solution.py:93
  225.5 3.4 copy-start.3
  248.1 40.2 %copy-start.5 = (f32[2048]{0:T(1024)S(1)}, f32[2048]{0:T(1024)}, u32[]{:S(2)}) copy-start(f32[2048]{0:T(1024)} %param.26) | copy-start | bytes 24580
  248.1 72.4 %all-gather.11.cloned.1.call-start = ((), (), s32[]{:S(2)}) async-start(), calls=%async_computation.7 | async-start | bytes 4718592 | tf_op jit(solution)/shard_map/all_gather | solution.py:102
  287.5 0.8 copy-start.4
  289.3 42.8 %copy-start.8 = (s32[1,256]{1,0:T(1,128)S(1)}, s32[1,256]{1,0:T(1,128)}, u32[]{:S(2)}) copy-start(s32[1,256]{1,0:T(1,128)} %param.28) | copy-start | bytes 3076
  289.3 43.6 %copy-start.9 = (s32[1,256]{1,0:T(1,128)S(1)}, s32[1,256]{1,0:T(1,128)}, u32[]{:S(2)}) copy-start(s32[1,256]{1,0:T(1,128)} %param.29) | copy-start | bytes 3076
  327.2 25.9 %all-to-all-start = ((bf16[8,128,768]{2,1,0:T(8,128)(2,1)}), bf16[8,128,768]{2,1,0:T(8,128)(2,1)}, u32[]{:S(2)}, u32[]{:S(2)}) async-start(bf16[8,128,768]{2,1,0:T(8,128)(2,1)} %bitcast.54), calls=%async_computation.1 | async-start | bytes 3145728 | tf_op jit(solution)/shard_map/all_to_all | solution.py:106
  354.7 1.2 copy-start.2
  359.7 24.4 %all-to-all-start.1 = ((bf16[16,1,8,4096]{3,2,1,0:T(8,128)(2,1)}), bf16[16,1,8,4096]{3,2,1,0:T(8,128)(2,1)}, u32[]{:S(2)}, u32[]{:S(2)}) async-start(bf16[16,1,8,4096]{3,2,1,0:T(8,128)(2,1)} %bitcast.52), calls=%async_computation.2 | async-start | bytes 2097152 | tf_op jit(solution)/shard_map/all_to_all | solution.py:117
Sparse Core Ops, SparseCore 0:
  10.7 80.9 all-gather.4
  94.4 77.8 all-gather.6
  194.1 31.3 all-gather.8
  248.2 37.7 reduce-scatter.1
  289.4 31.0 all-gather.10
where the time goes:
time: 396 us; the launch traced here: 395 us
  waiting for transfers between devices  271 us (68%)
  matrix products  50.8 us (13%)
  local copies, waits for them, and re-layouts  29.8 us (8%)
  other arithmetic  16.5 us (4%)
  between operations  15.3 us (4%)
  starting transfers between devices  11.7 us (3%)
    all_gather x1, waiting for transfers between devices, body(): key_rows = lax.all_gather(k_in, 'tok', axis=0, tiled=True)  75.5 us
    all_gather x1, waiting for transfers between devices, body(): value_rows = lax.all_gather(v_in, 'tok', axis=0, tiled=True)  63 us
    reduce_scatter x1, waiting for transfers between devices, body(): lax.psum_scatter(jnp.dot(hidden, down_weight, preferred_element_type=jnp....  37.9 us
    all_gather x1, waiting for transfers between devices, body(): gathered = lax.all_gather(residual_mid, 'req', axis=0, tiled=True)  31.3 us
    all_gather x1, waiting for transfers between devices, body(): lax.all_gather(next_normed, 'req', axis=0, tiled=True)  31.2 us
    all_to_all x1, waiting for transfers between devices, body(): lax.all_to_all(projected_cols, 'req', split_axis=0, concat_axis=1, tiled=...  18.2 us
    all_to_all x1, waiting for transfers between devices, body(): lax.all_to_all(outgoing, 'tok', split_axis=0, concat_axis=0, tiled=True)  14.1 us
    unnamed x26, local copies, waits for them, and re-layouts  12.8 us
  transfers between devices with their start and end apart: 7, of which 7 were waited for; matrix products, arithmetic and copies ran while one was open for 6% of the time, Pallas kernels for 0%

commit v1 on v0

--- a/solution.py
+++ b/solution.py
@@ -52,7 +52,11 @@
     query_split = q_in.reshape(row_count, HEADS, 2, head_dim)
     run_max = jnp.full((HEADS, 2, row_count), NEG_FILL, jnp.float32)
     key_rows = lax.all_gather(k_in, "tok", axis=0, tiled=True)
-    value_rows = lax.all_gather(v_in, "tok", axis=0, tiled=True)
+    size = lax.axis_size("tok")
+    repeats = [size if d == 0 else 1 for d in range(v_in.ndim)]
+    value_rows = lax.all_to_all(
+        jnp.tile(v_in, repeats), "tok", split_axis=0, concat_axis=0, tiled=True
+    )
     piece_len = key_rows.shape[0]
     key_split = key_rows.reshape(piece_len, HEADS, 2, head_dim)
     value_split = value_rows.reshape(piece_len, HEADS, 2 * head_dim)

time: 396 us -> 453 us (1.14)
  waiting for transfers between devices: 271 us -> 312 us
  local copies, waits for them, and re-layouts: 29.8 us -> 38.3 us
  starting transfers between devices: 11.7 us -> 19.6 us
    all_to_all x0 -> x1, waiting for transfers between devices: none -> 148 us  [body(): lax.all_to_all(jnp.tile(v_in, repeats), 'tok', split_axis=0, concat_axis=...]
    all_gather x1 -> x0, waiting for transfers between devices: 63 us -> none  [body(): value_rows = lax.all_gather(v_in, 'tok', axis=0, tiled=True)]
    all_gather x1, waiting for transfers between devices: 75.5 us -> 22.4 us  [body(): key_rows = lax.all_gather(k_in, 'tok', axis=0, tiled=True)]
    all_gather x1, waiting for transfers between devices: 31.3 us -> 39.5 us  [body(): gathered = lax.all_gather(residual_mid, 'req', axis=0, tiled=True)]
    all_to_all x0 -> x1, starting transfers between devices: none -> 8.14 us  [body(): lax.all_to_all(jnp.tile(v_in, repeats), 'tok', split_axis=0, concat_axis=...]
    another operation x0 -> x1, local copies, waits for them, and re-layouts: none -> 5.33 us  [body(): jnp.tile(v_in, repeats)]
where the time goes in v1:
time: 453 us; the launch traced here: 452 us
  waiting for transfers between devices  312 us (69%)
  matrix products  50.5 us (11%)
  local copies, waits for them, and re-layouts  38.3 us (8%)
  starting transfers between devices  19.6 us (4%)
  other arithmetic  16.4 us (4%)
  between operations  15.3 us (3%)
    all_to_all x1, waiting for transfers between devices, body(): lax.all_to_all(jnp.tile(v_in, repeats), 'tok', split_axis=0, concat_axis=...  148 us
    all_gather x1, waiting for transfers between devices, body(): gathered = lax.all_gather(residual_mid, 'req', axis=0, tiled=True)  39.5 us
    reduce_scatter x1, waiting for transfers between devices, body(): lax.psum_scatter(jnp.dot(hidden, down_weight, preferred_element_type=jnp....  37.9 us
    all_gather x1, waiting for transfers between devices, body(): lax.all_gather(next_normed, 'req', axis=0, tiled=True)  31.2 us
    all_gather x1, waiting for transfers between devices, body(): key_rows = lax.all_gather(k_in, 'tok', axis=0, tiled=True)  22.4 us
    all_to_all x1, waiting for transfers between devices, body(): lax.all_to_all(projected_cols, 'req', split_axis=0, concat_axis=1, tiled=...  18.2 us
    unnamed x26, local copies, waits for them, and re-layouts  16 us
    all_to_all x1, waiting for transfers between devices, body(): lax.all_to_all(outgoing, 'tok', split_axis=0, concat_axis=0, tiled=True)  14.1 us
  transfers between devices with their start and end apart: 7, of which 7 were waited for; matrix products, arithmetic and copies ran while one was open for 6% of the time, Pallas kernels for 0%

profile of v1, /device:TPU:0, one launch (start us, length us, event | category | flops | bytes accessed | tf_op | source)
XLA Modules:
  0.0 451.9 jit_solution(3771699204791995609)
XLA Ops:
  7.2 0.0 copy-start
  7.2 0.0 all-gather.4.cloned.1.call-start
  7.2 2.2 copy.33
  9.4 0.0 all-gather.4.cloned.1.call-update
  9.4 5.3 %tile.2 = bf16[16,128,2048]{2,1,0:T(8,128)(2,1)} broadcast(bf16[128,2048]{1,0:T(8,128)(2,1)} %param.18), dimensions={1,2} | broadcast | bytes 8912896 | tf_op jit(solution)/shard_map/tile | solution.py:58
  14.8 8.1 %all-to-all-start = ((bf16[16,128,2048]{2,1,0:T(8,128)(2,1)}), bf16[16,128,2048]{2,1,0:T(8,128)(2,1)}, u32[]{:S(2)}, u32[]{:S(2)}) async-start(bf16[16,128,2048]{2,1,0:T(8,128)(2,1)} %tile.2), calls=%async_computation | async-start | bytes 16777216 | tf_op jit(solution)/shard_map/all_to_all | solution.py:57
  22.9 0.0 all-gather.6.cloned.1.call-start
  23.0 2.2 reshape.104
  25.2 0.0 copy-done.7
  25.2 0.6 multiply_reduce_fusion.1
  27.2 0.0 copy-done.6
  27.2 0.4 fusion.30
  27.7 148.5 %all-to-all-done = bf16[16,128,2048]{2,1,0:T(8,128)(2,1)} async-done(((bf16[16,128,2048]{2,1,0:T(8,128)(2,1)}), bf16[16,128,2048]{2,1,0:T(8,128)(2,1)}, u32[]{:S(2)}, u32[]{:S(2)}) %all-to-all-start) | async-done | bytes 8388640 | tf_op jit(solution)/shard_map/all_to_all | solution.py:57
  176.1 10.4 %copy.45 = bf16[256,8,8,256]{3,2,1,0:T(8,128)(2,1)} copy(bf16[256,8,8,256]{3,1,2,0:T(8,128)(2,1)} %bitcast.21) | data formatting | bytes 16777216
  186.6 22.4 %all-gather.4.cloned.1.call-done = bf16[2048,2048]{0,1:T(8,128)(2,1)} async-done(((bf16[128,2048]{0,1:T(8,128)(2,1)}), bf16[2048,2048]{0,1:T(8,128)(2,1)}) %all-gather.4.cloned.1.call-update) | async-done | bytes 8388624 | tf_op jit(solution)/shard_map/all_gather | solution.py:54
  209.0 6.6 %fusion = (f32[8,2,128]{2,1,0:T(2,128)S(1)}, f32[8,2,128,2048]{3,2,1,0:T(8,128)S(1)}) fusion(pred[128,2048]{1,0:T(8,128)(4,1)S(1)} %fusion.30, bf16[2048,8,2,128]{0,3,2,1:T(8,128)(2,1)} %bitcast.48, bf16[128,8,2,128]{3,2,1,0:T(2,128)(2,1)} %reshape.104), kind=kOutput, calls=%fused_computation.5 | convolution fusion | flops 1086322688 | bytes 25960448 | tf_op jit(solution)/shard_map/qhmd,khmd->hmqk/dot_general | solution.py:68
  215.6 0.0 copy-start.1
  215.7 5.0 %fusion.1 = f32[8,2,128]{2,1,0:T(2,128)S(1)} fusion(f32[8,2,128,2048]{3,2,1,0:T(8,128)S(1)} %get-tuple-element.12, f32[8,2,128]{2,1,0:T(2,128)S(1)} %broadcast_maximum_fusion, pred[128,2048]{1,0:T(8,128)(4,1)S(1)} %fusion.30), kind=kLoop, calls=%fused_computation.6 | loop fusion | flops 20969472 | bytes 17055744 | tf_op jit(solution)/shard_map/reduce_sum | solution.py:74
  220.7 0.7 copy-done.1
  221.4 12.3 %fusion.15 = f32[8,2,128,256]{3,2,1,0:T(8,128)S(1)} fusion(bf16[2048,8,256,1]{2,1,0,3:T(8,128)(2,1)} %bitcast.49, f32[8,2,128,2048]{3,2,1,0:T(8,128)} %copy-done.1, f32[8,2,128]{2,1,0:T(2,128)S(1)} %broadcast_maximum_fusion, pred[128,2048]{1,0:T(8,128)(4,1)S(1)} %fusion.30, f32[8,2,128]{2,1,0:T(2,128)S(1)} %fusion.1), kind=kOutput, calls=%fused_computation.25 | convolution fusion | flops 2168979456 | bytes 27541504 | tf_op jit(solution)/shard_map/hmqk,khe->hmqe/dot_general | solution.py:75
  233.7 0.2 multiply_reduce_fusion
  233.9 1.1 fusion.31
  235.0 2.0 copy.37
  237.0 5.7 %fusion.14 = bf16[128,2048]{1,0:T(8,128)(2,1)} fusion(bf16[128,2048]{0,1:T(8,128)(2,1)} %bitcast.53, bf16[2048,2048]{1,0:T(8,128)(2,1)} %param.21, bf16[128,2048]{1,0:T(8,128)(2,1)} %param.15), kind=kOutput, calls=%fused_computation.23 | convolution fusion | flops 1074528256 | bytes 9961472 | tf_op jit(solution)/shard_map/dot_general | solution.py:90
  242.7 0.0 all-gather.6.cloned.1.call-update
  242.7 0.0 reduce-scatter.2.cloned.1.call-start
  242.8 39.5 %all-gather.6.cloned.1.call-done = bf16[1024,2048]{1,0:T(8,128)(2,1)} async-done(((bf16[128,2048]{1,0:T(8,128)(2,1)}), bf16[1024,2048]{1,0:T(8,128)(2,1)}) %all-gather.6.cloned.1.call-update) | async-done | bytes 4194320 | tf_op jit(solution)/shard_map/all_gather | solution.py:92
  282.3 3.2 fusion.3
  285.5 0.0 copy-done.10
  285.5 0.2 copy-done.3
  285.7 6.7 %fusion.21 = f32[1024,704]{0,1:T(8,128)} fusion(bf16[2048,704]{0,1:T(8,128)(2,1)} %param.23, bf16[1024,2048]{1,0:T(8,128)(2,1)S(1)} %copy-done.3, f32[2048]{0:T(1024)S(1)} %copy-done.10, f32[1024]{0:T(1024)S(1)} %add_rsqrt_fusion), kind=kOutput, calls=%fused_computation.28 | convolution fusion | flops 2961178624 | bytes 9973760 | tf_op jit(solution)/shard_map/dot_general | solution.py:94
  292.4 12.4 %convolution_convert_fusion = bf16[1024,2048]{1,0:T(8,128)(2,1)} fusion(bf16[704,2048]{1,0:T(8,128)(2,1)} %param.25, f32[1024,704]{0,1:T(8,128)} %fusion.21, bf16[2048,704]{0,1:T(8,128)(2,1)} %param.24, bf16[1024,2048]{1,0:T(8,128)(2,1)} %all-gather.6.cloned.1.call-done, f32[2048]{0:T(1024)S(1)} %copy-done.10, f32[1024]{0:T(1024)S(1)} %add_rsqrt_fusion), kind=kOutput, calls=%fused_computation.20 | convolution fusion | flops 5920391168 | bytes 17051648 | tf_op jit(solution)/shard_map/dot_general | solution.py:98
  304.8 0.0 reduce-scatter.2.cloned.1.call-update
  304.9 0.0 all-gather.8.cloned.1.call-start
  304.9 37.9 %reduce-scatter.2.cloned.1.call-done = bf16[128,2048]{1,0:T(8,128)(2,1)} async-done(((bf16[1024,2048]{1,0:T(8,128)(2,1)}), bf16[128,2048]{1,0:T(8,128)(2,1)}) %reduce-scatter.2.cloned.1.call-update) | async-done | bytes 524304 | tf_op jit(solution)/shard_map/reduce_scatter | solution.py:97
  342.8 1.5 fusion.25
  344.2 0.8 copy-done.4
  345.0 1.0 fusion.27
  346.0 0.0 all-gather.8.cloned.1.call-update
  346.0 0.0 copy-start.8
  346.0 0.0 copy-start.9
  346.1 31.2 %all-gather.8.cloned.1.call-done = bf16[1024,2048]{1,0:T(8,128)(2,1)} async-done(((bf16[128,2048]{1,0:T(8,128)(2,1)}), bf16[1024,2048]{1,0:T(8,128)(2,1)}) %all-gather.8.cloned.1.call-update) | async-done | bytes 4194320 | tf_op jit(solution)/shard_map/all_gather | solution.py:106
  377.2 6.8 %convolution_convert_fusion.1 = bf16[1024,768]{1,0:T(8,128)(2,1)} fusion(bf16[1024,2048]{1,0:T(8,128)(2,1)} %all-gather.8.cloned.1.call-done, bf16[2048,768]{1,0:T(8,128)(2,1)S(1)} %copy-done), kind=kOutput, calls=%fused_computation.24 | convolution fusion | flops 3222011904 | bytes 8912896 | tf_op jit(solution)/shard_map/dot_general | solution.py:105
  384.0 4.3 all-to-all-start.1
  388.3 0.5 broadcast.120
  388.8 0.7 reduce.9
  389.5 0.1 reshape_squeeze.6
  389.5 0.1 copy.39
  389.6 0.7 reduce.8
  390.3 0.1 reshape_squeeze.7
  390.4 1.2 sort.35
  391.7 18.2 %all-to-all-done.1 = bf16[8,128,768]{2,1,0:T(8,128)(2,1)} async-done(((bf16[8,128,768]{2,1,0:T(8,128)(2,1)}), bf16[8,128,768]{2,1,0:T(8,128)(2,1)}, u32[]{:S(2)}, u32[]{:S(2)}) %all-to-all-start.1) | async-done | bytes 1572896 | tf_op jit(solution)/shard_map/all_to_all | solution.py:110
  409.9 1.6 copy.44
  411.4 1.1 copy-done.2
  412.6 1.0 slice_bitcast_fusion
  413.6 2.8 gather_fusion
  416.5 7.0 %all-to-all-start.2 = ((bf16[16,1,8,4096]{3,2,1,0:T(8,128)(2,1)}), bf16[16,1,8,4096]{3,2,1,0:T(8,128)(2,1)}, u32[]{:S(2)}, u32[]{:S(2)}) async-start(bf16[16,1,8,4096]{3,2,1,0:T(8,128)(2,1)} %bitcast.52), calls=%async_computation.3 | async-start | bytes 2097152 | tf_op jit(solution)/shard_map/all_to_all | solution.py:121
  423.5 0.1 iota_select_fusion
  423.5 0.7 sort.34
  424.3 0.7 gather_fusion.1
  424.9 1.9 slice.42
  426.8 14.1 %all-to-all-done.2 = bf16[16,1,8,4096]{3,2,1,0:T(8,128)(2,1)} async-done(((bf16[16,1,8,4096]{3,2,1,0:T(8,128)(2,1)}), bf16[16,1,8,4096]{3,2,1,0:T(8,128)(2,1)}, u32[]{:S(2)}, u32[]{:S(2)}) %all-to-all-start.2) | async-done | bytes 1048608 | tf_op jit(solution)/shard_map/all_to_all | solution.py:121
  440.9 1.1 broadcast_in_dim.54
  442.0 3.4 scatter_fusion
  (28 shorter events, 0.1 us)
Async XLA Ops:
  7.2 370.1 %copy-start = (bf16[2048,768]{1,0:T(8,128)(2,1)S(1)}, bf16[2048,768]{1,0:T(8,128)(2,1)}, u32[]{:S(2)}) copy-start(bf16[2048,768]{1,0:T(8,128)(2,1)} %param.27) | copy-start | bytes 9437188
  7.2 201.8 %all-gather.4.cloned.1.call-start = ((), (), s32[]{:S(2)}) async-start(), calls=%async_computation.4 | async-start | bytes 8912896 | tf_op jit(solution)/shard_map/all_gather | solution.py:54
  14.8 10.4 %copy-start.7 = (f32[4,128]{1,0:T(4,128)S(1)}, f32[4,128]{1,0:T(4,128)}, u32[]{:S(2)}) copy-start(f32[4,128]{1,0:T(4,128)} %param.20) | copy-start | bytes 6148
  14.8 12.4 %copy-start.6 = (s32[1,2048]{1,0:T(1,128)S(1)}, s32[1,2048]{1,0:T(1,128)}, u32[]{:S(2)}) copy-start(s32[1,2048]{1,0:T(1,128)} %param.19) | copy-start | bytes 24580
  14.8 161.4 %all-to-all-start = ((bf16[16,128,2048]{2,1,0:T(8,128)(2,1)}), bf16[16,128,2048]{2,1,0:T(8,128)(2,1)}, u32[]{:S(2)}, u32[]{:S(2)}) async-start(bf16[16,128,2048]{2,1,0:T(8,128)(2,1)} %tile.2), calls=%async_computation | async-start | bytes 16777216 | tf_op jit(solution)/shard_map/all_to_all | solution.py:57
  22.9 259.3 %all-gather.6.cloned.1.call-start = ((), (), s32[]{:S(2)}) async-start(), calls=%async_computation.5 | async-start | bytes 4718592 | tf_op jit(solution)/shard_map/all_gather | solution.py:92
  215.6 5.7 %copy-start.1 = (f32[8,2,128,2048]{3,2,1,0:T(8,128)}, f32[8,2,128,2048]{3,2,1,0:T(8,128)S(1)}, u32[]{:S(2)}) copy-start(f32[8,2,128,2048]{3,2,1,0:T(8,128)S(1)} %get-tuple-element.12) | copy-start | bytes 50331652
  242.7 42.8 %copy-start.10 = (f32[2048]{0:T(1024)S(1)}, f32[2048]{0:T(1024)}, u32[]{:S(2)}) copy-start(f32[2048]{0:T(1024)} %param.22) | copy-start | bytes 24580
  242.7 100.0 %reduce-scatter.2.cloned.1.call-start = ((), (), s32[]{:S(2)}) async-start(), calls=%async_computation.6 | async-start | bytes 4718592 | tf_op jit(solution)/shard_map/reduce_scatter | solution.py:97
  282.3 3.4 copy-start.3
  304.8 40.2 %copy-start.5 = (f32[2048]{0:T(1024)S(1)}, f32[2048]{0:T(1024)}, u32[]{:S(2)}) copy-start(f32[2048]{0:T(1024)} %param.26) | copy-start | bytes 24580
  304.9 72.4 %all-gather.8.cloned.1.call-start = ((), (), s32[]{:S(2)}) async-start(), calls=%async_computation.7 | async-start | bytes 4718592 | tf_op jit(solution)/shard_map/all_gather | solution.py:106
  344.2 0.8 copy-start.4
  346.0 42.8 %copy-start.8 = (s32[1,256]{1,0:T(1,128)S(1)}, s32[1,256]{1,0:T(1,128)}, u32[]{:S(2)}) copy-start(s32[1,256]{1,0:T(1,128)} %param.28) | copy-start | bytes 3076
  346.0 43.6 %copy-start.9 = (s32[1,256]{1,0:T(1,128)S(1)}, s32[1,256]{1,0:T(1,128)}, u32[]{:S(2)}) copy-start(s32[1,256]{1,0:T(1,128)} %param.29) | copy-start | bytes 3076
  384.0 25.9 %all-to-all-start.1 = ((bf16[8,128,768]{2,1,0:T(8,128)(2,1)}), bf16[8,128,768]{2,1,0:T(8,128)(2,1)}, u32[]{:S(2)}, u32[]{:S(2)}) async-start(bf16[8,128,768]{2,1,0:T(8,128)(2,1)} %bitcast.54), calls=%async_computation.2 | async-start | bytes 3145728 | tf_op jit(solution)/shard_map/all_to_all | solution.py:110
  411.4 1.2 copy-start.2
  416.5 24.4 %all-to-all-start.2 = ((bf16[16,1,8,4096]{3,2,1,0:T(8,128)(2,1)}), bf16[16,1,8,4096]{3,2,1,0:T(8,128)(2,1)}, u32[]{:S(2)}, u32[]{:S(2)}) async-start(bf16[16,1,8,4096]{3,2,1,0:T(8,128)(2,1)} %bitcast.52), calls=%async_computation.3 | async-start | bytes 2097152 | tf_op jit(solution)/shard_map/all_to_all | solution.py:121
Sparse Core Ops, SparseCore 0:
  10.7 198.2 all-gather.3
  242.8 39.3 all-gather.5
  305.0 37.7 reduce-scatter.1
  346.2 31.0 all-gather.7
